TPU v7x, 32 devices: a whole 2x2x4 slice. The times are simulated.
32 devices in a mesh: groups: 2 (over x), ctx: 16 (over z, y, core).
Axes of the slice: x: 2, y: 2, z: 4, core: 2. Of those that a mesh axis runs over, the one named last changes fastest.
Arguments:
- query_input: bfloat16 [32, 1536], P('groups'), parts along dimension 0, may hold values from -20 to 20
- query_gain: bfloat16 [1536], replicated, may hold values from 0.5 to 1.5
- nope_weight: bfloat16 [1536, 4096], P(None, 'ctx'), may hold values from -0.15625 to 0.15625
- rope_weight: bfloat16 [1536, 2048], P(None, 'ctx'), may hold values from -0.15625 to 0.15625
- key_up: bfloat16 [32, 128, 512], P('ctx'), may hold values from -0.5 to 0.5
- value_up: bfloat16 [32, 512, 128], P('ctx'), may hold values from -1 to 1
- out_weight: bfloat16 [4096, 7168], P('ctx'), may hold values from -0.09375 to 0.09375
- cache_latent: bfloat16 [4, 32768, 512], P('groups', 'ctx'), parts along dimension 0, may hold values from -8 to 8
- cache_rope: bfloat16 [4, 64, 32768], P('groups', None, 'ctx'), parts along dimension 0, may hold values from -256 to 256
- cached_length: int32 [4], P('groups'), parts along dimension 0, may hold values from 16384 to 32760, as said below
Outputs:
- attn_out: bfloat16 [32, 7168], P('groups'), parts along dimension 0
There are 2 independent parts, one for each index of `groups`. A program takes and returns all parts, laid end to end along the dimension named above; an argument that names none is the same for every part. Nothing has to cross between parts.
Inputs may be any that keep to these rules, and one draw needn't show every extreme that they name: `cached_length`: in every part one request has exactly 32760, so that its last new token sees the cache's last position.
All inputs are finite; a program needn't handle non-finite values.
Results may differ from a plain program's by a relative error of at most 0.012.
Values may be sent and summed in bfloat16 or wider, within the bound.
A program may use at most 128 MiB of HBM per device.

v0:
```python
import math

import jax
import jax.numpy as jnp
from jax import lax
from jax.sharding import PartitionSpec as P

mscale_yarn = 1.0 + 0.1 * math.log(40.0)
masked_score = -1e30


def attend_heads(
    latent_query, rope_query, cache_latent, cache_rope, cached_length, positions, softmax_scale
):
    row_count, head_count, latent_width = latent_query.shape
    rope_width = rope_query.shape[2]
    requests = cache_latent.shape[0]
    stretch_rows = row_count // requests
    peak_list, sum_list, pool_list = ([], [], [])
    for request in range(requests):
        flat_latent = latent_query[request * stretch_rows : (request + 1) * stretch_rows].reshape(
            stretch_rows * head_count, latent_width
        )
        flat_rope = rope_query[request * stretch_rows : (request + 1) * stretch_rows].reshape(
            stretch_rows * head_count, rope_width
        )
        scores = jnp.einsum(
            "ql,pl->qp", flat_latent, cache_latent[request], preferred_element_type=jnp.float32
        )
        scores = (
            scores + jnp.dot(flat_rope, cache_rope[request], preferred_element_type=jnp.float32)
        ) * softmax_scale
        last_seen = (
            cached_length[request]
            + jnp.arange(stretch_rows * head_count, dtype=jnp.int32) // head_count
        )
        visible = positions[None, :] <= last_seen[:, None]
        scores = jnp.where(visible, scores, masked_score)
        block_peak = jnp.max(scores, axis=1)
        weights = jnp.where(visible, jnp.exp(scores - block_peak[:, None]), 0.0)
        block_sum = jnp.sum(weights, axis=1)
        block_pool = jnp.dot(
            weights.astype(jnp.bfloat16), cache_latent[request], preferred_element_type=jnp.float32
        )
        peak_list.append(block_peak.reshape(stretch_rows, head_count))
        sum_list.append(block_sum.reshape(stretch_rows, head_count))
        pool_list.append(block_pool.reshape(stretch_rows, head_count, latent_width))
    return (
        jnp.concatenate(peak_list, axis=0),
        jnp.concatenate(sum_list, axis=0),
        jnp.concatenate(pool_list, axis=0),
    )


def project_heads(pooled, weight_sum, value_up, out_weight):
    attended = (pooled / weight_sum[:, :, None]).astype(jnp.bfloat16)
    head_values = jnp.einsum(
        "rhl,hlv->rhv", attended, value_up, preferred_element_type=jnp.float32
    ).astype(jnp.bfloat16)
    return jnp.dot(
        head_values.reshape(head_values.shape[0], -1),
        out_weight,
        preferred_element_type=jnp.float32,
    )


def local(
    query_input,
    query_gain,
    nope_weight,
    rope_weight,
    key_up,
    value_up,
    out_weight,
    cache_latent,
    cache_rope,
    cached_length,
):
    head_local = key_up.shape[0]
    nope_width = key_up.shape[1]
    rope_width = rope_weight.shape[1] // head_local
    row_count = query_input.shape[0]
    key_count = cache_latent.shape[1]
    widened = query_input.astype(jnp.float32)
    normed = (
        widened
        * lax.rsqrt(jnp.mean(widened * widened, axis=-1, keepdims=True) + 1e-06)
        * query_gain.astype(jnp.float32)
    ).astype(jnp.bfloat16)
    query_nope = (
        jnp.dot(normed, nope_weight, preferred_element_type=jnp.float32)
        .astype(jnp.bfloat16)
        .reshape(row_count, head_local, nope_width)
    )
    query_rope = (
        jnp.dot(normed, rope_weight, preferred_element_type=jnp.float32)
        .astype(jnp.bfloat16)
        .reshape(row_count, head_local, rope_width)
    )
    query_latent = jnp.einsum(
        "rhn,hnl->rhl", query_nope, key_up, preferred_element_type=jnp.float32
    ).astype(jnp.bfloat16)
    softmax_scale = mscale_yarn * mscale_yarn / math.sqrt(nope_width + rope_width)
    positions = lax.axis_index("ctx") * key_count + jnp.arange(key_count, dtype=jnp.int32)
    every_latent, every_rope = (
        lax.all_gather(query_latent, "ctx", axis=1, tiled=True),
        lax.all_gather(query_rope, "ctx", axis=1, tiled=True),
    )
    block_peak, block_sum, block_pool = attend_heads(
        every_latent, every_rope, cache_latent, cache_rope, cached_length, positions, softmax_scale
    )
    pooled_in = lax.all_to_all(block_pool[None], "ctx", split_axis=2, concat_axis=0, tiled=True)
    peak_in = lax.all_to_all(block_peak[None], "ctx", split_axis=2, concat_axis=0, tiled=True)
    sum_in = lax.all_to_all(block_sum[None], "ctx", split_axis=2, concat_axis=0, tiled=True)
    row_top = jnp.max(peak_in, axis=0)
    factor = jnp.exp(peak_in - row_top[None])
    pooled = jnp.sum(pooled_in * factor[..., None], axis=0)
    weight_sum = jnp.sum(sum_in * factor, axis=0)
    partial_value = project_heads(pooled, weight_sum, value_up, out_weight)
    return lax.psum(partial_value, "ctx").astype(jnp.bfloat16)


def solution(mesh):
    placed = (
        P("groups", None),
        P(),
        P(None, "ctx"),
        P(None, "ctx"),
        P("ctx", None, None),
        P("ctx", None, None),
        P("ctx", None),
        P("groups", "ctx", None),
        P("groups", None, "ctx"),
        P("groups"),
    )
    return jax.shard_map(
        local, mesh=mesh, in_specs=placed, out_specs=P("groups", None), check_vma=False
    )
```

profile of v0, /device:TPU:0, one launch (start us, length us, event | category | flops | bytes accessed | tf_op | source)
XLA Modules:
  0.0 175.1 jit_solution(12115778293265833145)
XLA Ops:
  0.0 1.4 fusion.44
  1.4 0.7 convert_element_type.40
  2.1 0.9 fusion.28
  3.1 1.1 fusion.21
  4.1 1.1 fusion.20
  5.2 24.6 %all_gather.6 = bf16[16,32,512]{2,0,1:T(8,128)(2,1)S(1)} all-gather(bf16[16,2,512]{2,0,1:T(8,128)(2,1)S(1)} %fusion.20), channel_id=1, replica_groups=mesh['groups'=2,'ctx'=16] {'ctx'}, dimensions={1}, use_global_device_ids=true | all-gather | bytes 557056 | tf_op jit(solution)/shard_map/all_gather | solution.py:106
  30.0 0.2 convolution_convert_fusion.3
  30.3 17.8 %all_gather.7 = bf16[16,32,64]{2,0,1:T(8,128)(2,1)S(1)} all-gather(bf16[16,2,64]{2,0,1:T(8,128)(2,1)S(1)} %copy.64), channel_id=1, replica_groups=mesh['groups'=2,'ctx'=16] {'ctx'}, dimensions={1}, use_global_device_ids=true | all-gather | bytes 69632 | tf_op jit(solution)/shard_map/all_gather | solution.py:107
  48.2 2.5 %fusion.6 = f32[256,2048]{1,0:T(8,128)S(1)} fusion(bf16[256,512]{1,0:T(8,128)(2,1)S(1)} %bitcast.80, bf16[2,2048,512]{2,1,0:T(8,128)(2,1)} %param.17), kind=kOutput, calls=%fused_computation.10 | convolution fusion | flops 536870912 | bytes 4456448 | tf_op jit(solution)/shard_map/ql,pl->qp/dot_general | solution.py:27
  50.7 0.3 copy-done.1
  51.0 0.7 fusion.10
  51.8 1.3 broadcast_add_fusion
  53.1 0.6 fusion.46
  53.8 0.6 fusion.45
  54.4 1.0 fusion.16
  55.6 0.7 copy.72
  56.3 3.5 %all-to-all-start.2 = ((f32[1,16,32]{1,0,2:T(1,128)}), f32[1,16,32]{1,0,2:T(1,128)S(1)}, u32[]{:S(2)}, u32[]{:S(2)}) async-start(f32[1,16,32]{1,0,2:T(1,128)} %copy.72), calls=%async_computation.2 | async-start | bytes 32768 | tf_op jit(solution)/shard_map/all_to_all | solution.py:114
  60.0 2.4 %fusion.4 = f32[8,32,512]{2,1,0:T(8,128)S(1)} fusion(bf16[8,32,2048]{2,1,0:T(8,128)(2,1)S(1)} %bitcast.79, bf16[2,2048,512]{2,1,0:T(8,128)(2,1)} %param.17), kind=kOutput, calls=%fused_computation.8 | convolution fusion | flops 536870912 | bytes 3670016 | tf_op jit(solution)/shard_map/dot_general | solution.py:42
  62.4 0.4 copy-done.2
  62.8 0.7 fusion.8
  63.5 0.7 copy.70
  64.2 2.1 %all-to-all-done.2 = f32[1,16,32]{1,0,2:T(1,128)S(1)} async-done(((f32[1,16,32]{1,0,2:T(1,128)}), f32[1,16,32]{1,0,2:T(1,128)S(1)}, u32[]{:S(2)}, u32[]{:S(2)}) %all-to-all-start.2) | async-done | bytes 2080 | tf_op jit(solution)/shard_map/all_to_all | solution.py:114
  66.3 3.9 %all-to-all-start.1 = ((f32[1,16,32]{1,0,2:T(1,128)}), f32[1,16,32]{1,0,2:T(1,128)S(1)}, u32[]{:S(2)}, u32[]{:S(2)}) async-start(f32[1,16,32]{1,0,2:T(1,128)} %copy.70), calls=%async_computation.1 | async-start | bytes 32768 | tf_op jit(solution)/shard_map/all_to_all | solution.py:113
  70.3 1.6 copy.68
  71.9 4.8 %all-to-all-done.1 = f32[1,16,32]{1,0,2:T(1,128)S(1)} async-done(((f32[1,16,32]{1,0,2:T(1,128)}), f32[1,16,32]{1,0,2:T(1,128)S(1)}, u32[]{:S(2)}, u32[]{:S(2)}) %all-to-all-start.1) | async-done | bytes 2080 | tf_op jit(solution)/shard_map/all_to_all | solution.py:113
  76.7 3.7 %all-to-all-start = ((f32[1,16,32,512]{3,1,0,2:T(8,128)}), f32[1,16,32,512]{3,1,0,2:T(8,128)S(1)}, u32[]{:S(2)}, u32[]{:S(2)}) async-start(f32[1,16,32,512]{3,1,0,2:T(8,128)} %copy.68), calls=%async_computation | async-start | bytes 2097152 | tf_op jit(solution)/shard_map/all_to_all | solution.py:112
  80.4 0.2 copy.71
  80.6 22.6 %all-to-all-done = f32[1,16,32,512]{3,1,0,2:T(8,128)S(1)} async-done(((f32[1,16,32,512]{3,1,0,2:T(8,128)}), f32[1,16,32,512]{3,1,0,2:T(8,128)S(1)}, u32[]{:S(2)}, u32[]{:S(2)}) %all-to-all-start) | async-done | bytes 1048608 | tf_op jit(solution)/shard_map/all_to_all | solution.py:112
  103.2 1.1 fusion.23
  104.3 0.2 fusion.22
  104.5 2.6 %fusion.36 = f32[16,7168]{1,0:T(8,128)S(1)} fusion(bf16[256,7168]{1,0:T(8,128)(2,1)} %param.16, bf16[2,2,8,128]{3,2,1,0:T(8,128)(2,1)S(1)} %fusion.22), kind=kOutput, calls=%fused_computation.48 | convolution fusion | flops 58720256 | bytes 4136960 | tf_op jit(solution)/shard_map/dot_general | solution.py:60
  107.1 68.0 %all-reduce.1 = bf16[16,7168]{1,0:T(8,128)(2,1)} all-reduce(f32[16,7168]{1,0:T(8,128)S(1)} %fusion.36), channel_id=1, replica_groups=mesh['groups'=2,'ctx'=16] {'ctx'}, use_global_device_ids=true, to_apply=%region_8.9 | all-reduce | flops 114688 | bytes 688128 | tf_op jit(solution)/shard_map/psum | solution.py:120
  (31 shorter events, 0.8 us)
Async XLA Ops:
  0.0 3.1 %copy-start = (bf16[1536,256]{1,0:T(8,128)(2,1)S(1)}, bf16[1536,256]{1,0:T(8,128)(2,1)}, u32[]{:S(2)}) copy-start(bf16[1536,256]{1,0:T(8,128)(2,1)} %param.12) | copy-start | bytes 2359300
  0.0 30.0 %copy-start.4 = (bf16[16,1536]{1,0:T(8,128)(2,1)S(1)}, bf16[16,1536]{1,0:T(8,128)(2,1)}, u32[]{:S(2)}) copy-start(bf16[16,1536]{1,0:T(8,128)(2,1)} %param.10) | copy-start | bytes 147460
  0.0 30.0 %copy-start.5 = (bf16[1536,128]{1,0:T(8,128)(2,1)S(1)}, bf16[1536,128]{1,0:T(8,128)(2,1)}, u32[]{:S(2)}) copy-start(bf16[1536,128]{1,0:T(8,128)(2,1)} %param.13) | copy-start | bytes 1179652
  48.2 2.8 %copy-start.1 = (bf16[2,2048,512]{2,1,0:T(8,128)(2,1)S(1)}, bf16[2,2048,512]{2,1,0:T(8,128)(2,1)}, u32[]{:S(2)}) copy-start(bf16[2,2048,512]{2,1,0:T(8,128)(2,1)} %param.17) | copy-start | bytes 12582916
  51.0 2.1 %copy-start.3 = (bf16[2,64,2048]{2,1,0:T(8,128)(2,1)S(1)}, bf16[2,64,2048]{2,1,0:T(8,128)(2,1)}, u32[]{:S(2)}) copy-start(bf16[2,64,2048]{2,1,0:T(8,128)(2,1)} %param.18) | copy-start | bytes 1572868
  56.3 10.0 %all-to-all-start.2 = ((f32[1,16,32]{1,0,2:T(1,128)}), f32[1,16,32]{1,0,2:T(1,128)S(1)}, u32[]{:S(2)}, u32[]{:S(2)}) async-start(f32[1,16,32]{1,0,2:T(1,128)} %copy.72), calls=%async_computation.2 | async-start | bytes 32768 | tf_op jit(solution)/shard_map/all_to_all | solution.py:114
  60.0 2.8 %copy-start.2 = (bf16[2,2048,512]{2,1,0:T(8,128)(2,1)S(1)}, bf16[2,2048,512]{2,1,0:T(8,128)(2,1)}, u32[]{:S(2)}) copy-start(bf16[2,2048,512]{2,1,0:T(8,128)(2,1)} %param.17) | copy-start | bytes 12582916
  66.3 10.4 %all-to-all-start.1 = ((f32[1,16,32]{1,0,2:T(1,128)}), f32[1,16,32]{1,0,2:T(1,128)S(1)}, u32[]{:S(2)}, u32[]{:S(2)}) async-start(f32[1,16,32]{1,0,2:T(1,128)} %copy.70), calls=%async_computation.1 | async-start | bytes 32768 | tf_op jit(solution)/shard_map/all_to_all | solution.py:113
  71.9 32.4 %copy-start.6 = (bf16[2,512,128]{2,1,0:T(8,128)(2,1)S(1)}, bf16[2,512,128]{2,1,0:T(8,128)(2,1)}, u32[]{:S(2)}) copy-start(bf16[2,512,128]{2,1,0:T(8,128)(2,1)} %param.15) | copy-start | bytes 786436
  76.7 26.5 %all-to-all-start = ((f32[1,16,32,512]{3,1,0,2:T(8,128)}), f32[1,16,32,512]{3,1,0,2:T(8,128)S(1)}, u32[]{:S(2)}, u32[]{:S(2)}) async-start(f32[1,16,32,512]{3,1,0,2:T(8,128)} %copy.68), calls=%async_computation | async-start | bytes 2097152 | tf_op jit(solution)/shard_map/all_to_all | solution.py:112
where the time goes:
time: 176 us; the launch traced here: 175 us
  blocking collectives  110 us (62%)
  waiting for transfers between devices  29.5 us (17%)
  matrix products  12.8 us (7%)
  starting transfers between devices  11 us (6%)
  local copies, waits for them, and re-layouts  5.92 us (3%)
  other arithmetic  5.27 us (3%)
    psum x1, blocking collectives, local(): return lax.psum(partial_value, 'ctx').astype(jnp.bfloat16)  68 us
    all_gather x1, blocking collectives, local(): lax.all_gather(query_latent, 'ctx', axis=1, tiled=True)  24.6 us
    all_to_all x1, waiting for transfers between devices, local(): lax.all_to_all(block_pool[None], 'ctx', split_axis=2, concat_axis=0, tile...  22.6 us
    all_gather x1, blocking collectives, local(): lax.all_gather(query_rope, 'ctx', axis=1, tiled=True)  17.8 us
    all_to_all x1, waiting for transfers between devices, local(): lax.all_to_all(block_peak[None], 'ctx', split_axis=2, concat_axis=0, tile...  4.8 us
    all_to_all x1, starting transfers between devices, local(): lax.all_to_all(block_peak[None], 'ctx', split_axis=2, concat_axis=0, tile...  3.88 us
    all_to_all x1, starting transfers between devices, local(): lax.all_to_all(block_pool[None], 'ctx', split_axis=2, concat_axis=0, tile...  3.65 us
  transfers between devices with their start and end apart: 3, of which 3 were waited for; matrix products, arithmetic and copies ran while one was open for 3% of the time, Pallas kernels for 0%

commit v1 on v0

v1 whole, which is shorter than its diff:
```python
import functools
import math

import jax
import jax.numpy as jnp
from jax import lax
from jax.experimental import pallas as pl
from jax.experimental.pallas import tpu as pltpu
from jax.sharding import PartitionSpec as P

mscale_yarn = 1.0 + 0.1 * math.log(40.0)
masked_score = -1e30
MESH = pl.DeviceIdType.MESH
F32 = jnp.float32
BF16 = jnp.bfloat16
NT = (((1,), (1,)), ((), ()))


def kernel(
    n, tile,
    x_hbm, gain_ref, nope_hbm, ropew_hbm, kup_hbm, vup_hbm, outw_hbm, lat_hbm, crope_hbm, len_ref,
    out_ref,
    x_v, nope_v, ropew_v, kup_v, vup_v, outw_v, lat_v, crope_v,
    qbuf, score_s, peak_s, sum_s, pool_s, pk_buf, sm_buf,
    sb1, rb1, sb2, rb2, sb3, rb3,
    opart, ob1, or1, os2, or2, os3, or3, fin,
    ld_sem,
    q1s, q1r, q2s, q2r, q3s, q3r,
    pks, pkr, sms, smr,
    p1s, p1r, p2s, p2r, p3s, p3r,
    o1s, o1r, o2s, o2r, o3s, o3r,
    f1s, f1r, f2s, f2r, f3s, f3r,
):
    me = lax.axis_index("ctx")
    outer = n // 4
    a, y, c = me // 4, (me // 2) % 2, me % 2
    heads, nope_w, lat_w = kup_v.shape
    rows = x_v.shape[0]
    requests, keys, _ = lat_v.shape
    stretch = rows // requests
    block_rows = heads * stretch
    rope_all = ropew_v.shape[1]
    rope_w = rope_all // heads
    scale = mscale_yarn * mscale_yarn / math.sqrt(nope_w + rope_w)

    def dev(ai, yi, ci):
        return ai * 4 + yi * 2 + ci

    def far(k):
        return (a + k) % outer

    def back(k):
        return (a + outer - k) % outer

    def remote(src, dst, ssem, rsem, target):
        return pltpu.make_async_remote_copy(
            src_ref=src, dst_ref=dst, send_sem=ssem, recv_sem=rsem,
            device_id={"ctx": target}, device_id_type=MESH,
        )

    loads = []

    def load(src, dst):
        copy = pltpu.make_async_copy(src, dst, ld_sem.at[len(loads)])
        copy.start()
        loads.append(copy)
        return copy

    load_x = load(x_hbm, x_v)
    load_nope = load(nope_hbm, nope_v)
    load_rope = load(ropew_hbm, ropew_v)
    load_kup = load(kup_hbm, kup_v)
    load_cache = [load(lat_hbm, lat_v)]
    for h in range(heads):
        load_cache.append(load(crope_hbm, crope_v.at[:, h * rope_w : (h + 1) * rope_w, :]))
    load_vup = load(vup_hbm, vup_v)
    load_outw = load(outw_hbm, outw_v)

    barrier = pltpu.get_barrier_semaphore()
    for k in range(1, n):
        pl.semaphore_signal(
            barrier, inc=1, device_id={"ctx": (me + k) % n}, device_id_type=MESH
        )

    load_x.wait()
    widened = x_v[...].astype(F32)
    normed = (
        widened
        * lax.rsqrt(jnp.mean(widened * widened, axis=-1, keepdims=True) + 1e-06)
        * gain_ref[...]
    ).astype(BF16)
    load_nope.wait()
    query_nope = jnp.dot(normed, nope_v[...], preferred_element_type=F32).astype(BF16)
    load_rope.wait()
    query_rope = jnp.dot(normed, ropew_v[...], preferred_element_type=F32)
    load_kup.wait()
    latents = [
        jnp.dot(
            query_nope[:, h * nope_w : (h + 1) * nope_w], kup_v[h], preferred_element_type=F32
        )
        for h in range(heads)
    ]
    lane_head = lax.broadcasted_iota(jnp.int32, (stretch, rope_all), 1) // rope_w
    for b in range(requests):
        part = slice(b * stretch, (b + 1) * stretch)
        qbuf[me, b, :, :lat_w] = jnp.concatenate([t[part] for t in latents], axis=0).astype(BF16)
        qbuf[me, b, :, lat_w:] = jnp.concatenate(
            [jnp.where(lane_head == h, query_rope[part], 0.0) for h in range(heads)], axis=0
        ).astype(BF16)
    pl.semaphore_wait(barrier, n - 1)

    pending = []

    def send(copy):
        copy.start()
        pending.append(copy)

    def gather(at, s1, r1, s2, r2, s3, r3):
        def to_far(k):
            ref = at(a, y, c)
            return remote(ref, ref, s1.at[k], r1.at[k], dev(far(k), y, c))

        def from_far(k):
            ref = at(back(k), y, c)
            return remote(ref, ref, s1.at[k], r1.at[k], dev(far(k), y, c))

        def to_y(k, yy):
            ref = at(back(k), yy, c)
            return remote(ref, ref, s2.at[k], r2.at[k], dev(a, 1 - y, c))

        def to_core(k, j, cc):
            ref = at(back(k), (y + j) % 2, cc)
            return remote(ref, ref, s3.at[2 * k + j], r3.at[2 * k + j], dev(a, y, 1 - c))

        for k in range(1, outer):
            send(to_far(k))
        send(to_y(0, y))
        send(to_core(0, 0, c))
        for k in range(1, outer):
            from_far(k).wait_recv()
            send(to_y(k, y))
            send(to_core(k, 0, c))
            to_y(k - 1, 1 - y).wait_recv()
            send(to_core(k - 1, 1, c))
        to_y(outer - 1, 1 - y).wait_recv()
        send(to_core(outer - 1, 1, c))
        for k in range(outer):
            for j in range(2):
                to_core(k, j, 1 - c).wait_recv()

    gather(lambda ai, yi, ci: qbuf.at[dev(ai, yi, ci)], q1s, q1r, q2s, q2r, q3s, q3r)

    for copy in load_cache:
        copy.wait()
    first_key = me * keys
    tile_devs = tile // block_rows
    tiles_per = n // tile_devs
    tiles = requests * tiles_per

    def each_tile(body):
        if tiles <= 2:
            for t in range(tiles):
                body(t, t // tiles_per, (t % tiles_per) * tile_devs, t * tile)
        else:
            def step(t, carry):
                body(
                    t, t // tiles_per, (t % tiles_per) * tile_devs,
                    pl.multiple_of(t * tile, tile),
                )
                return carry
            lax.fori_loop(0, tiles, step, 0)

    def compact(column):
        return jnp.transpose(jnp.broadcast_to(column, (tile, 128)))[0:1, :]

    def spread(row):
        return jnp.transpose(jnp.broadcast_to(row, (128, tile)))[:, 0:1]

    def scores_of(t, b, d0, r0):
        query = qbuf[pl.ds(d0, tile_devs), b].reshape(tile, lat_w + rope_all)
        raw = lax.dot_general(query[:, :lat_w], lat_v[b], NT, preferred_element_type=F32)
        raw = raw + jnp.dot(query[:, lat_w:], crope_v[b], preferred_element_type=F32)
        row = lax.broadcasted_iota(jnp.int32, (tile, 1), 0) % stretch
        limit = len_ref[b] + row - first_key
        where_key = lax.broadcasted_iota(jnp.int32, (tile, keys), 1)
        raw = jnp.where(where_key <= limit, raw, masked_score)
        score_s[t] = raw
        peak = jnp.max(raw, axis=1, keepdims=True)
        peak_s[pl.ds(r0, tile), :] = jnp.broadcast_to(peak, (tile, 128))
        pk_buf[me, :, pl.ds(r0, tile)] = compact(peak)

    each_tile(scores_of)

    def share(buf, ss, rs):
        for k in range(1, n):
            send(remote(buf.at[me], buf.at[me], ss.at[k], rs.at[k], (me + k) % n))

    def shared(buf, ss, rs):
        for k in range(1, n):
            ref = buf.at[(me + n - k) % n]
            remote(ref, ref, ss.at[k], rs.at[k], (me + k) % n).wait_recv()

    share(pk_buf, pks, pkr)

    def pool_of(t, b, d0, r0):
        peak = peak_s[pl.ds(r0, tile), 0:1]
        weights = jnp.exp((score_s[t] - peak) * scale)
        sum_s[pl.ds(r0, tile), :] = jnp.broadcast_to(
            jnp.sum(weights, axis=1, keepdims=True), (tile, 128)
        )
        pool_s[b, pl.ds(d0, tile_devs)] = jnp.dot(
            weights.astype(BF16), lat_v[b], preferred_element_type=F32
        ).reshape(tile_devs, block_rows, lat_w)

    each_tile(pool_of)
    shared(pk_buf, pks, pkr)

    def rescale(t, b, d0, r0):
        top = jnp.max(pk_buf[:, :, pl.ds(r0, tile)], axis=0)
        factor = jnp.exp((peak_s[pl.ds(r0, tile), 0:1] - spread(top)) * scale)
        sm_buf[me, :, pl.ds(r0, tile)] = compact(sum_s[pl.ds(r0, tile), 0:1] * factor)
        scaled = pool_s[b, pl.ds(d0, tile_devs)].reshape(tile, lat_w) * factor
        scaled = scaled.reshape(tile_devs, block_rows, lat_w)
        pool_s[b, pl.ds(d0, tile_devs)] = scaled
        sb1[pl.ds(d0, tile_devs), b] = scaled.astype(BF16)

    each_tile(rescale)

    def to_core(ka, j):
        slot = 2 * ka + j
        return remote(
            sb1.at[dev(far(ka), (y + j) % 2, 1 - c)], rb1.at[slot],
            p1s.at[slot], p1r.at[slot], dev(a, y, 1 - c),
        )

    def to_y(ka):
        return remote(sb2.at[ka], rb2.at[ka], p2s.at[ka], p2r.at[ka], dev(a, 1 - y, c))

    def to_far(ka):
        return remote(sb3.at[ka], rb3.at[ka], p3s.at[ka], p3r.at[ka], dev(far(ka), y, c))

    order = list(range(1, outer)) + [0]
    for j in (1, 0):
        for ka in order:
            send(to_core(ka, j))
    share(sm_buf, sms, smr)
    for ka in order:
        to_core(ka, 1).wait_recv()
        d = dev(far(ka), 1 - y, c)
        sb2[ka] = (pool_s[:, d] + rb1[2 * ka + 1].astype(F32)).astype(BF16)
        send(to_y(ka))
    for ka in order:
        to_core(ka, 0).wait_recv()
        to_y(ka).wait_recv()
        total = pool_s[:, dev(far(ka), y, c)] + rb1[2 * ka].astype(F32) + rb2[ka].astype(F32)
        if ka:
            sb3[ka] = total.astype(BF16)
            send(to_far(ka))
    for ka in range(1, outer):
        to_far(ka).wait_recv()
        total = total + rb3[ka].astype(F32)
    shared(sm_buf, sms, smr)

    all_sums = jnp.sum(sm_buf[...], axis=0)
    per_request = n * block_rows
    owner = lax.broadcasted_iota(jnp.int32, (block_rows, per_request), 1)
    mine = owner == me * block_rows + lax.broadcasted_iota(
        jnp.int32, (block_rows, per_request), 0
    )
    attended = []
    for b in range(requests):
        sums = jnp.sum(
            jnp.where(mine, all_sums[:, b * per_request : (b + 1) * per_request], 0.0),
            axis=1, keepdims=True,
        )
        attended.append(total[b] / sums)
    load_vup.wait()
    values = []
    for h in range(heads):
        stacked = jnp.concatenate(
            [t[h * stretch : (h + 1) * stretch] for t in attended], axis=0
        ).astype(BF16)
        values.append(jnp.dot(stacked, vup_v[h], preferred_element_type=F32).astype(BF16))
    head_values = jnp.concatenate(values, axis=1)

    half = rows // 2
    width = opart.shape[3]
    model = out_ref.shape[1]

    def to_core_out(q):
        return remote(ob1.at[q, 1 - c], or1.at[q], o1s.at[q], o1r.at[q], dev(a, y, 1 - c))

    def to_y_out(ka):
        return remote(os2.at[ka], or2.at[ka], o2s.at[ka], o2r.at[ka], dev(a, 1 - y, c))

    def to_far_out(ka):
        return remote(os3.at[ka], or3.at[ka], o3s.at[ka], o3r.at[ka], dev(far(ka), y, c))

    load_outw.wait()
    for q in range(n // 2):
        used = max(0, min(width, model - q * width))
        if used < width:
            opart[q] = jnp.zeros((2, half, width), F32)
            ob1[q] = jnp.zeros((2, half, width), BF16)
        if used:
            partial = jnp.dot(
                head_values, outw_v[:, q * width : q * width + used], preferred_element_type=F32
            )
            for side in range(2):
                piece = partial[side * half : (side + 1) * half]
                opart[q, side, :, :used] = piece
                ob1[q, side, :, :used] = piece.astype(BF16)
        send(to_core_out(q))
    for ka in order:
        q = far(ka) * 2 + (1 - y)
        to_core_out(q).wait_recv()
        os2[ka] = (opart[q, c] + or1[q].astype(F32)).astype(BF16)
        send(to_y_out(ka))
    for ka in order:
        q = far(ka) * 2 + y
        to_core_out(q).wait_recv()
        to_y_out(ka).wait_recv()
        summed = opart[q, c] + or1[q].astype(F32) + or2[ka].astype(F32)
        if ka:
            os3[ka] = summed.astype(BF16)
            send(to_far_out(ka))
    for ka in range(1, outer):
        to_far_out(ka).wait_recv()
        summed = summed + or3[ka].astype(F32)
    fin[a * 2 + y, c] = summed.astype(BF16)
    gather(lambda ai, yi, ci: fin.at[ai * 2 + yi, ci], f1s, f1r, f2s, f2r, f3s, f3r)

    for q in range(n // 2):
        used = max(0, min(width, model - q * width))
        if used:
            out_ref[:, q * width : q * width + used] = jnp.concatenate(
                [fin[q, 0, :, :used].astype(F32), fin[q, 1, :, :used].astype(F32)], axis=0
            ).astype(BF16)
    for copy in pending:
        copy.wait_send()


def local(
    n, query_input, query_gain, nope_weight, rope_weight, key_up, value_up, out_weight,
    cache_latent, cache_rope, cached_length,
):
    heads, nope_w, lat_w = key_up.shape
    rows = query_input.shape[0]
    requests, keys, _ = cache_latent.shape
    stretch = rows // requests
    block_rows = heads * stretch
    rope_all = rope_weight.shape[1]
    rope_w = rope_all // heads
    model = out_weight.shape[1]
    outer = n // 4
    flat = requests * n * block_rows
    tile = min(256, n * block_rows)
    half = rows // 2
    lane_tiles = -(-model // 128)
    width = -(-lane_tiles // (n // 2)) * 128
    block = (requests, block_rows, lat_w)
    vmem = pltpu.VMEM
    dma = lambda count: pltpu.SemaphoreType.DMA((count,))
    any_spec = pl.BlockSpec(memory_space=pl.ANY)
    vmem_spec = pl.BlockSpec(memory_space=pltpu.VMEM)
    gather_sems = [dma(outer)] * 4 + [dma(2 * outer)] * 2
    return pl.pallas_call(
        functools.partial(kernel, n, tile),
        out_shape=jax.ShapeDtypeStruct((rows, model), BF16),
        in_specs=[any_spec, vmem_spec] + [any_spec] * 7
        + [pl.BlockSpec(memory_space=pltpu.SMEM)],
        out_specs=vmem_spec,
        scratch_shapes=[
            vmem(query_input.shape, BF16), vmem(nope_weight.shape, BF16),
            vmem(rope_weight.shape, BF16), vmem(key_up.shape, BF16),
            vmem(value_up.shape, BF16), vmem(out_weight.shape, BF16),
            vmem(cache_latent.shape, BF16), vmem((requests, rope_all, keys), BF16),
            vmem((n, requests, block_rows, lat_w + rope_all), BF16),
            vmem((flat // tile, tile, keys), F32),
            vmem((flat, 128), F32), vmem((flat, 128), F32),
            vmem((requests, n, block_rows, lat_w), F32),
            vmem((n, 1, flat), F32), vmem((n, 1, flat), F32),
            vmem((n, *block), BF16), vmem((n // 2, *block), BF16),
            vmem((outer, *block), BF16), vmem((outer, *block), BF16),
            vmem((outer, *block), BF16), vmem((outer, *block), BF16),
            vmem((n // 2, 2, half, width), F32), vmem((n // 2, 2, half, width), BF16),
            vmem((n // 2, half, width), BF16),
            vmem((outer, half, width), BF16), vmem((outer, half, width), BF16),
            vmem((outer, half, width), BF16), vmem((outer, half, width), BF16),
            vmem((n // 2, 2, half, width), BF16),
            dma(7 + heads),
            *gather_sems,
            dma(n), dma(n), dma(n), dma(n),
            dma(n // 2), dma(n // 2), dma(outer), dma(outer), dma(outer), dma(outer),
            dma(n // 2), dma(n // 2), dma(outer), dma(outer), dma(outer), dma(outer),
            *gather_sems,
        ],
        compiler_params=pltpu.CompilerParams(
            collective_id=0, has_side_effects=True, vmem_limit_bytes=63 * 1024 * 1024
        ),
    )(
        query_input, query_gain.astype(F32).reshape(1, -1), nope_weight, rope_weight, key_up,
        value_up, out_weight, cache_latent, cache_rope, cached_length,
    )


def solution(mesh):
    placed = (
        P("groups", None),
        P(),
        P(None, "ctx"),
        P(None, "ctx"),
        P("ctx", None, None),
        P("ctx", None, None),
        P("ctx", None),
        P("groups", "ctx", None),
        P("groups", None, "ctx"),
        P("groups"),
    )
    return jax.shard_map(
        functools.partial(local, mesh.shape["ctx"]), mesh=mesh, in_specs=placed,
        out_specs=P("groups", None), check_vma=False,
    )
```

time: 176 us -> 57.3 us (0.33)
  blocking collectives: 110 us -> 0 us
  Pallas kernels: 0 us -> 54.1 us
  waiting for transfers between devices: 29.5 us -> 0 us
  matrix products: 12.8 us -> 0 us
  starting transfers between devices: 11 us -> 0 us
  other arithmetic: 5.27 us -> 0 us
  local copies, waits for them, and re-layouts: 5.92 us -> 2.92 us
    psum x1 -> x0, blocking collectives: 68 us -> none  [local(): return lax.psum(partial_value, 'ctx').astype(jnp.bfloat16)]
    pallas_call x0 -> x1, Pallas kernels: none -> 54.1 us  [local(): pl.pallas_call(functools.partial(kernel, n, tile), out_shape=jax.ShapeDty...]
    all_gather x2 -> x0, blocking collectives: 42.4 us -> none  [the longest x1 24.6 us: local(): lax.all_gather(query_latent, 'ctx', axis=1, tiled=True)]
    all_to_all x3 -> x0, waiting for transfers between devices: 29.5 us -> none  [the longest x1 22.6 us: local(): lax.all_to_all(block_pool[None], 'ctx', split_axis=2, concat_axis=0, tile...]
    dot_general x11 -> x0, matrix products: 12.8 us -> none  [the longest x2 3.21 us: attend_heads(): jnp.einsum('ql,pl->qp', flat_latent, cache_latent[request], preferred_ele...]
    all_to_all x3 -> x0, starting transfers between devices: 11 us -> none  [the longest x1 3.88 us: local(): lax.all_to_all(block_peak[None], 'ctx', split_axis=2, concat_axis=0, tile...]
    reduce_sum x4 -> x0, other arithmetic: 3.1 us -> none  [the longest x1 1.11 us: local(): pooled = jnp.sum(pooled_in * factor[..., None], axis=0)]
    broadcast_in_dim x3 -> x0, local copies, waits for them, and re-layouts: 2.97 us -> none  [the longest x1 1.6 us: local(): block_pool[None]]
  transfers between devices with their start and end apart: 3 -> 0, of which waited for: 3 -> 0; matrix products, arithmetic and copies ran while one was open for 3% -> 0% of each run, Pallas kernels for 0% -> 0%
where the time goes in v1:
time: 57.3 us; the launch traced here: 57 us
  Pallas kernels  54.1 us (94%)
  local copies, waits for them, and re-layouts  2.92 us (5%)
    pallas_call x1, Pallas kernels, local(): pl.pallas_call(functools.partial(kernel, n, tile), out_shape=jax.ShapeDty...  54.1 us
    unnamed x1, local copies, waits for them, and re-layouts  1.64 us
    reshape x1, local copies, waits for them, and re-layouts, local(): query_gain.astype(F32).reshape(1, -1)  1.28 us

profile of v1, /device:TPU:0, one launch (start us, length us, event | category | flops | bytes accessed | tf_op | source)
XLA Modules:
  0.0 57.0 jit_solution(10140898768190516283)
XLA Ops:
  0.0 1.3 %reshape.8.gain_ref = f32[1,1536]{1,0:T(1,128)} reshape(bf16[1536]{0:T(1024)(128)(2,1)} %param.11) | data formatting | bytes 9216 | tf_op jit(solution)/shard_map/reshape | solution.py:402
  1.3 54.1 %shard_map.100 = bf16[16,7168]{1,0:T(8,128)(2,1)} custom-call(bf16[16,1536]{1,0:T(8,128)(2,1)} %x_hbm.1, f32[1,1536]{1,0:T(1,128)} %reshape.8.gain_ref, bf16[1536,256]{1,0:T(8,128)(2,1)} %nope_hbm.1, bf16[1536,128]{1,0:T(8,128)(2,1)} %ropew_hbm.1, bf16[2,128,512]{2,1,0:T(8,128)(2,1)} %kup_hbm.1, bf16[2,512,128]{2,1,0:T(8,128)(2,1)} %vup_hbm.1, ...), custom_call_target="tpu_custom_call" | custom-call | tf_op jit(solution)/shard_map/pallas_call | solution.py:367
  55.4 1.6 %copy.12 = bf16[16,7168]{1,0:T(8,128)(2,1)} copy(bf16[16,7168]{1,0:T(8,128)(2,1)} %shard_map.100) | data formatting | bytes 458752

commit v2 on v1

--- a/solution.py
+++ b/solution.py
@@ -22,18 +22,18 @@
     out_ref,
     x_v, nope_v, ropew_v, kup_v, vup_v, outw_v, lat_v, crope_v,
     qbuf, score_s, peak_s, sum_s, pool_s, pk_buf, sm_buf,
-    sb1, rb1, sb2, rb2, sb3, rb3,
-    opart, ob1, or1, os2, or2, os3, or3, fin,
+    sb1, rb1, sb2, rb2,
+    opart, ob1, or1, os2, or2, fin,
     ld_sem,
-    q1s, q1r, q2s, q2r, q3s, q3r,
+    q1s, q1r, q2s, q2r,
     pks, pkr, sms, smr,
-    p1s, p1r, p2s, p2r, p3s, p3r,
-    o1s, o1r, o2s, o2r, o3s, o3r,
-    f1s, f1r, f2s, f2r, f3s, f3r,
+    p1s, p1r, p2s, p2r,
+    o1s, o1r, o2s, o2r,
+    f1s, f1r, f2s, f2r,
 ):
     me = lax.axis_index("ctx")
-    outer = n // 4
-    a, y, c = me // 4, (me // 2) % 2, me % 2
+    chips = n // 2
+    chip, c = me // 2, me % 2
     heads, nope_w, lat_w = kup_v.shape
     rows = x_v.shape[0]
     requests, keys, _ = lat_v.shape
@@ -43,14 +43,12 @@
     rope_w = rope_all // heads
     scale = mscale_yarn * mscale_yarn / math.sqrt(nope_w + rope_w)
 
-    def dev(ai, yi, ci):
-        return ai * 4 + yi * 2 + ci
-
-    def far(k):
-        return (a + k) % outer
-
-    def back(k):
-        return (a + outer - k) % outer
+    def peer(k):
+        flipped, bit = 0, 1
+        while bit < chips:
+            flipped = flipped + ((chip // bit + (k // bit) % 2) % 2) * bit
+            bit *= 2
+        return flipped
 
     def remote(src, dst, ssem, rsem, target):
         return pltpu.make_async_remote_copy(
@@ -70,12 +68,6 @@
     load_nope = load(nope_hbm, nope_v)
     load_rope = load(ropew_hbm, ropew_v)
     load_kup = load(kup_hbm, kup_v)
-    load_cache = [load(lat_hbm, lat_v)]
-    for h in range(heads):
-        load_cache.append(load(crope_hbm, crope_v.at[:, h * rope_w : (h + 1) * rope_w, :]))
-    load_vup = load(vup_hbm, vup_v)
-    load_outw = load(outw_hbm, outw_v)
-
     barrier = pltpu.get_barrier_semaphore()
     for k in range(1, n):
         pl.semaphore_signal(
@@ -87,13 +79,18 @@
     normed = (
         widened
         * lax.rsqrt(jnp.mean(widened * widened, axis=-1, keepdims=True) + 1e-06)
-        * gain_ref[...]
+        * gain_ref[...].astype(F32).reshape(1, -1)
     ).astype(BF16)
     load_nope.wait()
     query_nope = jnp.dot(normed, nope_v[...], preferred_element_type=F32).astype(BF16)
     load_rope.wait()
     query_rope = jnp.dot(normed, ropew_v[...], preferred_element_type=F32)
     load_kup.wait()
+    load_cache = [load(lat_hbm, lat_v)]
+    for h in range(heads):
+        load_cache.append(load(crope_hbm, crope_v.at[:, h * rope_w : (h + 1) * rope_w, :]))
+    load_vup = load(vup_hbm, vup_v)
+    load_outw = load(outw_hbm, outw_v)
     latents = [
         jnp.dot(
             query_nope[:, h * nope_w : (h + 1) * nope_w], kup_v[h], preferred_element_type=F32
@@ -115,40 +112,25 @@
         copy.start()
         pending.append(copy)
 
-    def gather(at, s1, r1, s2, r2, s3, r3):
-        def to_far(k):
-            ref = at(a, y, c)
-            return remote(ref, ref, s1.at[k], r1.at[k], dev(far(k), y, c))
-
-        def from_far(k):
-            ref = at(back(k), y, c)
-            return remote(ref, ref, s1.at[k], r1.at[k], dev(far(k), y, c))
-
-        def to_y(k, yy):
-            ref = at(back(k), yy, c)
-            return remote(ref, ref, s2.at[k], r2.at[k], dev(a, 1 - y, c))
-
-        def to_core(k, j, cc):
-            ref = at(back(k), (y + j) % 2, cc)
-            return remote(ref, ref, s3.at[2 * k + j], r3.at[2 * k + j], dev(a, y, 1 - c))
-
-        for k in range(1, outer):
-            send(to_far(k))
-        send(to_y(0, y))
-        send(to_core(0, 0, c))
-        for k in range(1, outer):
-            from_far(k).wait_recv()
-            send(to_y(k, y))
-            send(to_core(k, 0, c))
-            to_y(k - 1, 1 - y).wait_recv()
-            send(to_core(k - 1, 1, c))
-        to_y(outer - 1, 1 - y).wait_recv()
-        send(to_core(outer - 1, 1, c))
-        for k in range(outer):
-            for j in range(2):
-                to_core(k, j, 1 - c).wait_recv()
-
-    gather(lambda ai, yi, ci: qbuf.at[dev(ai, yi, ci)], q1s, q1r, q2s, q2r, q3s, q3r)
+    def gather(at, s1, r1, s2, r2):
+        def to_chip(k, source):
+            ref = at(source, c)
+            return remote(ref, ref, s1.at[k], r1.at[k], peer(k) * 2 + c)
+
+        def to_core(k, side):
+            ref = at(peer(k), side)
+            return remote(ref, ref, s2.at[k], r2.at[k], chip * 2 + 1 - c)
+
+        for k in range(1, chips):
+            send(to_chip(k, chip))
+        send(to_core(0, c))
+        for k in range(1, chips):
+            to_chip(k, peer(k)).wait_recv()
+            send(to_core(k, c))
+        for k in range(chips):
+            to_core(k, 1 - c).wait_recv()
+
+    gather(lambda at_chip, side: qbuf.at[at_chip * 2 + side], q1s, q1r, q2s, q2r)
 
     for copy in load_cache:
         copy.wait()
@@ -226,39 +208,27 @@
 
     each_tile(rescale)
 
-    def to_core(ka, j):
-        slot = 2 * ka + j
+    def to_core(k):
         return remote(
-            sb1.at[dev(far(ka), (y + j) % 2, 1 - c)], rb1.at[slot],
-            p1s.at[slot], p1r.at[slot], dev(a, y, 1 - c),
-        )
-
-    def to_y(ka):
-        return remote(sb2.at[ka], rb2.at[ka], p2s.at[ka], p2r.at[ka], dev(a, 1 - y, c))
-
-    def to_far(ka):
-        return remote(sb3.at[ka], rb3.at[ka], p3s.at[ka], p3r.at[ka], dev(far(ka), y, c))
-
-    order = list(range(1, outer)) + [0]
-    for j in (1, 0):
-        for ka in order:
-            send(to_core(ka, j))
+            sb1.at[peer(k) * 2 + 1 - c], rb1.at[k], p1s.at[k], p1r.at[k], chip * 2 + 1 - c
+        )
+
+    def to_chip(k):
+        return remote(sb2.at[k], rb2.at[k], p2s.at[k], p2r.at[k], peer(k) * 2 + c)
+
+    order = list(range(1, chips)) + [0]
+    for k in order:
+        send(to_core(k))
     share(sm_buf, sms, smr)
-    for ka in order:
-        to_core(ka, 1).wait_recv()
-        d = dev(far(ka), 1 - y, c)
-        sb2[ka] = (pool_s[:, d] + rb1[2 * ka + 1].astype(F32)).astype(BF16)
-        send(to_y(ka))
-    for ka in order:
-        to_core(ka, 0).wait_recv()
-        to_y(ka).wait_recv()
-        total = pool_s[:, dev(far(ka), y, c)] + rb1[2 * ka].astype(F32) + rb2[ka].astype(F32)
-        if ka:
-            sb3[ka] = total.astype(BF16)
-            send(to_far(ka))
-    for ka in range(1, outer):
-        to_far(ka).wait_recv()
-        total = total + rb3[ka].astype(F32)
+    for k in order:
+        to_core(k).wait_recv()
+        total = pool_s[:, peer(k) * 2 + c] + rb1[k].astype(F32)
+        if k:
+            sb2[k] = total.astype(BF16)
+            send(to_chip(k))
+    for k in range(1, chips):
+        to_chip(k).wait_recv()
+        total = total + rb2[k].astype(F32)
     shared(sm_buf, sms, smr)
 
     all_sums = jnp.sum(sm_buf[...], axis=0)
@@ -288,16 +258,15 @@
     model = out_ref.shape[1]
 
     def to_core_out(q):
-        return remote(ob1.at[q, 1 - c], or1.at[q], o1s.at[q], o1r.at[q], dev(a, y, 1 - c))
-
-    def to_y_out(ka):
-        return remote(os2.at[ka], or2.at[ka], o2s.at[ka], o2r.at[ka], dev(a, 1 - y, c))
-
-    def to_far_out(ka):
-        return remote(os3.at[ka], or3.at[ka], o3s.at[ka], o3r.at[ka], dev(far(ka), y, c))
+        return remote(
+            ob1.at[q, 1 - c], or1.at[q], o1s.at[q], o1r.at[q], chip * 2 + 1 - c
+        )
+
+    def to_chip_out(k):
+        return remote(os2.at[k], or2.at[k], o2s.at[k], o2r.at[k], peer(k) * 2 + c)
 
     load_outw.wait()
-    for q in range(n // 2):
+    for q in range(chips):
         used = max(0, min(width, model - q * width))
         if used < width:
             opart[q] = jnp.zeros((2, half, width), F32)
@@ -311,26 +280,20 @@
                 opart[q, side, :, :used] = piece
                 ob1[q, side, :, :used] = piece.astype(BF16)
         send(to_core_out(q))
-    for ka in order:
-        q = far(ka) * 2 + (1 - y)
+    for k in order:
+        q = peer(k)
         to_core_out(q).wait_recv()
-        os2[ka] = (opart[q, c] + or1[q].astype(F32)).astype(BF16)
-        send(to_y_out(ka))
-    for ka in order:
-        q = far(ka) * 2 + y
-        to_core_out(q).wait_recv()
-        to_y_out(ka).wait_recv()
-        summed = opart[q, c] + or1[q].astype(F32) + or2[ka].astype(F32)
-        if ka:
-            os3[ka] = summed.astype(BF16)
-            send(to_far_out(ka))
-    for ka in range(1, outer):
-        to_far_out(ka).wait_recv()
-        summed = summed + or3[ka].astype(F32)
-    fin[a * 2 + y, c] = summed.astype(BF16)
-    gather(lambda ai, yi, ci: fin.at[ai * 2 + yi, ci], f1s, f1r, f2s, f2r, f3s, f3r)
-
-    for q in range(n // 2):
+        summed = opart[q, c] + or1[q].astype(F32)
+        if k:
+            os2[k] = summed.astype(BF16)
+            send(to_chip_out(k))
+    for k in range(1, chips):
+        to_chip_out(k).wait_recv()
+        summed = summed + or2[k].astype(F32)
+    fin[chip, c] = summed.astype(BF16)
+    gather(lambda at_chip, side: fin.at[at_chip, side], f1s, f1r, f2s, f2r)
+
+    for q in range(chips):
         used = max(0, min(width, model - q * width))
         if used:
             out_ref[:, q * width : q * width + used] = jnp.concatenate(
@@ -352,18 +315,18 @@
     rope_all = rope_weight.shape[1]
     rope_w = rope_all // heads
     model = out_weight.shape[1]
-    outer = n // 4
+    chips = n // 2
     flat = requests * n * block_rows
     tile = min(256, n * block_rows)
     half = rows // 2
     lane_tiles = -(-model // 128)
-    width = -(-lane_tiles // (n // 2)) * 128
+    width = -(-lane_tiles // chips) * 128
     block = (requests, block_rows, lat_w)
     vmem = pltpu.VMEM
     dma = lambda count: pltpu.SemaphoreType.DMA((count,))
     any_spec = pl.BlockSpec(memory_space=pl.ANY)
     vmem_spec = pl.BlockSpec(memory_space=pltpu.VMEM)
-    gather_sems = [dma(outer)] * 4 + [dma(2 * outer)] * 2
+    sems = [dma(chips)] * 4
     return pl.pallas_call(
         functools.partial(kernel, n, tile),
         out_shape=jax.ShapeDtypeStruct((rows, model), BF16),
@@ -380,26 +343,19 @@
             vmem((flat, 128), F32), vmem((flat, 128), F32),
             vmem((requests, n, block_rows, lat_w), F32),
             vmem((n, 1, flat), F32), vmem((n, 1, flat), F32),
-            vmem((n, *block), BF16), vmem((n // 2, *block), BF16),
-            vmem((outer, *block), BF16), vmem((outer, *block), BF16),
-            vmem((outer, *block), BF16), vmem((outer, *block), BF16),
-            vmem((n // 2, 2, half, width), F32), vmem((n // 2, 2, half, width), BF16),
-            vmem((n // 2, half, width), BF16),
-            vmem((outer, half, width), BF16), vmem((outer, half, width), BF16),
-            vmem((outer, half, width), BF16), vmem((outer, half, width), BF16),
-            vmem((n // 2, 2, half, width), BF16),
+            vmem((n, *block), BF16), vmem((chips, *block), BF16),
+            vmem((chips, *block), BF16), vmem((chips, *block), BF16),
+            vmem((chips, 2, half, width), F32), vmem((chips, 2, half, width), BF16),
+            vmem((chips, half, width), BF16), vmem((chips, half, width), BF16),
+            vmem((chips, half, width), BF16), vmem((chips, 2, half, width), BF16),
             dma(7 + heads),
-            *gather_sems,
-            dma(n), dma(n), dma(n), dma(n),
-            dma(n // 2), dma(n // 2), dma(outer), dma(outer), dma(outer), dma(outer),
-            dma(n // 2), dma(n // 2), dma(outer), dma(outer), dma(outer), dma(outer),
-            *gather_sems,
+            *sems, dma(n), dma(n), dma(n), dma(n), *sems, *sems, *sems,
         ],
         compiler_params=pltpu.CompilerParams(
             collective_id=0, has_side_effects=True, vmem_limit_bytes=63 * 1024 * 1024
         ),
     )(
-        query_input, query_gain.astype(F32).reshape(1, -1), nope_weight, rope_weight, key_up,
+        query_input, query_gain, nope_weight, rope_weight, key_up,
         value_up, out_weight, cache_latent, cache_rope, cached_length,
     )
 

time: 57.3 us -> 48.8 us (0.85)
  Pallas kernels: 54.1 us -> 46.9 us
  local copies, waits for them, and re-layouts: 2.92 us -> 1.64 us
    pallas_call x1, Pallas kernels: 54.1 us -> 46.9 us  [local(): pl.pallas_call(functools.partial(kernel, n, tile), out_shape=jax.ShapeDty...]
    reshape x1 -> x0, local copies, waits for them, and re-layouts: 1.28 us -> none  [local(): query_gain.astype(F32).reshape(1, -1)]
where the time goes in v2:
time: 48.8 us; the launch traced here: 48.6 us
  Pallas kernels  46.9 us (96%)
  local copies, waits for them, and re-layouts  1.64 us (3%)
    pallas_call x1, Pallas kernels, local(): pl.pallas_call(functools.partial(kernel, n, tile), out_shape=jax.ShapeDty...  46.9 us
    unnamed x1, local copies, waits for them, and re-layouts  1.64 us

profile of v2, /device:TPU:0, one launch (start us, length us, event | category | flops | bytes accessed | tf_op | source)
XLA Modules:
  0.0 48.6 jit_solution(11680912916828563981)
XLA Ops:
  0.0 46.9 %shard_map.100 = bf16[16,7168]{1,0:T(8,128)(2,1)} custom-call(bf16[16,1536]{1,0:T(8,128)(2,1)} %x_hbm.1, bf16[1536]{0:T(1024)(128)(2,1)} %gain_ref.1, bf16[1536,256]{1,0:T(8,128)(2,1)} %nope_hbm.1, bf16[1536,128]{1,0:T(8,128)(2,1)} %ropew_hbm.1, bf16[2,128,512]{2,1,0:T(8,128)(2,1)} %kup_hbm.1, bf16[2,512,128]{2,1,0:T(8,128)(2,1)} %vup_hbm.1, ...), custom_call_target="tpu_custom_call" | custom-call | tf_op jit(solution)/shard_map/pallas_call | solution.py:330
  46.9 1.6 %copy.12 = bf16[16,7168]{1,0:T(8,128)(2,1)} copy(bf16[16,7168]{1,0:T(8,128)(2,1)} %shard_map.100) | data formatting | bytes 458752
